TPU v7x, 32 devices: a whole 2x2x4 slice. The times are simulated.
32 devices in a mesh: groups: 2 (over y), seq: 4 (over z), tp: 2 (over x), kv: 2 (over core).
Axes of the slice: x: 2, y: 2, z: 4, core: 2. Of those that a mesh axis runs over, the one named last changes fastest.
Arguments:
- events: bfloat16 [8, 512, 2048], P('groups', 'seq', ('tp', 'kv')), parts along dimension 0, may hold values from -6 to 6
- history_cache: bfloat16 [2, 8, 512, 1024], P(None, ('groups', 'seq'), None, ('tp', 'kv')), parts along dimension 1, may hold values from -6 to 6
- block_counts: int32 [8], P(('groups', 'seq')), parts along dimension 0, may hold values from 1 to 4
- semantic_ids: int32 [4, 128], P(None, ('groups', 'seq')), parts along dimension 1, may hold values from 0 to 4095
- beam_parents: int32 [3, 128], P(None, ('groups', 'seq')), parts along dimension 1, may hold values from 0 to 15
- query_weight: bfloat16 [2048, 2048], P('seq', ('tp', 'kv')), may hold values from -0.125 to 0.125
- keyval_weight: bfloat16 [2, 2048, 1024], P(None, 'seq', ('tp', 'kv')), may hold values from -0.125 to 0.125
- out_weight: bfloat16 [2048, 2048], P('seq', ('tp', 'kv')), may hold values from -0.125 to 0.125
- cross_weight: bfloat16 [2, 2048, 1024], P(None, 'seq', ('tp', 'kv')), may hold values from -0.125 to 0.125
- decoder_query: bfloat16 [2048, 2048], P(None, ('tp', 'kv')), may hold values from -0.125 to 0.125
- decoder_out: bfloat16 [2048, 2048], P(None, ('tp', 'kv')), may hold values from -0.125 to 0.125
- code_table: bfloat16 [4096, 2048], P(('tp', 'kv')), may hold values from -6 to 6
- encoder_gain: float32 [2048], replicated, may hold values from 0.25 to 1.75
- cross_gain: float32 [2048], replicated, may hold values from 0.25 to 1.75
- decoder_gain: float32 [2048], replicated, may hold values from 0.25 to 1.75
Outputs:
- encoded: bfloat16 [8, 512, 2048], P(('groups', 'seq'), ('tp', 'kv')), parts along dimension 0
- beam_state: bfloat16 [128, 2048], P(('groups', 'seq'), ('tp', 'kv')), parts along dimension 0
There are 2 independent parts, one for each index of `groups`. A program takes and returns all parts, laid end to end along the dimension named above; an argument that names none is the same for every part. Nothing has to cross between parts.
Inputs may be any that keep to these rules, and one draw needn't show every extreme that they name: A user's first 128 * block_counts new events are real; the rest are padding. `semantic_ids`: the codebook entry decoded for each beam row. `beam_parents`: the beam of the previous step that each beam row continues, counted among its user's 16 beams.
All inputs are finite; a program needn't handle non-finite values.
Results may differ from a plain program's by a relative error of at most 0.014.
Values may be sent and summed in bfloat16 or wider, within the bound.
A program may use at most 64 MiB of HBM per device.

v0:
```python
import jax
import jax.numpy as jnp
from jax import lax
from jax.sharding import PartitionSpec as P

H = 16
DH = 128
KVH = 8
BLK = 128
STEPS = 4
eps = 1e-06


def root_norm(values, scale_gain):
    mean_square = jnp.mean(values * values, axis=-1, keepdims=True)
    return values * lax.rsqrt(mean_square + eps) * scale_gain


def shards(
    events,
    history_cache,
    block_counts,
    semantic_ids,
    beam_parents,
    query_weight,
    keyval_weight,
    out_weight,
    cross_weight,
    decoder_query,
    decoder_out,
    code_table,
    encoder_gain,
    cross_gain,
    decoder_gain,
):
    head_size = DH
    group_ratio = H // KVH
    relayed = lax.all_to_all(events, "seq", split_axis=0, concat_axis=1, tiled=True)
    whole = lax.all_gather(relayed, ("tp", "kv"), axis=2, tiled=True)
    users = whole.shape[0]
    length = whole.shape[1]
    width = whole.shape[2]
    source = whole.reshape(users * length, width).astype(jnp.float32)
    normed = root_norm(source, encoder_gain).astype(jnp.bfloat16)
    query_cols = query_weight.shape[1]
    key_cols = keyval_weight.shape[2]
    joined = jnp.concatenate([query_weight, keyval_weight[0], keyval_weight[1]], axis=1)
    projected = jnp.dot(
        normed,
        lax.all_gather(joined, "seq", axis=0, tiled=True),
        preferred_element_type=jnp.float32,
    )
    queries = projected[:, :query_cols].astype(jnp.bfloat16)
    keys_new = projected[:, query_cols : query_cols + key_cols].astype(jnp.bfloat16)
    values_new = projected[:, query_cols + key_cols :].astype(jnp.bfloat16)
    out_full, cross_full = (
        lax.all_gather(out_weight, "seq", axis=0, tiled=True),
        lax.all_gather(cross_weight, "seq", axis=1, tiled=True),
    )
    key_groups = key_cols // head_size
    history_len = history_cache.shape[2]
    query_heads = queries.reshape(users, length, key_groups, group_ratio, head_size)
    key_heads = jnp.concatenate(
        [history_cache[0], keys_new.reshape(users, length, key_cols)], axis=1
    )
    key_heads = key_heads.reshape(users, history_len + length, key_groups, head_size)
    value_heads = jnp.concatenate(
        [history_cache[1], values_new.reshape(users, length, key_cols)], axis=1
    )
    value_heads = value_heads.reshape(users, history_len + length, key_groups, head_size)
    scores = jnp.einsum(
        "uigad,ujgd->ugaij", query_heads, key_heads, preferred_element_type=jnp.float32
    ) * head_size ** (-0.5)
    query_index = lax.broadcasted_iota(jnp.int32, (length, history_len + length), 0)
    key_index = lax.broadcasted_iota(jnp.int32, (length, history_len + length), 1) - history_len
    live_limit = (block_counts * BLK)[:, None, None, None, None]
    visible = (key_index < 0)[None, None, None] | (key_index <= query_index)[None, None, None] & (
        key_index[None, None, None] < live_limit
    )
    raised = jnp.where(visible, jnp.exp(scores), jnp.float32(0.0))
    denominator = jnp.sum(raised, axis=-1, keepdims=True)
    softened = (raised / denominator).astype(jnp.bfloat16)
    attended = jnp.einsum(
        "ugaij,ujgd->uigad", softened, value_heads, preferred_element_type=jnp.float32
    )
    attended = attended.astype(jnp.bfloat16).reshape(users * length, query_cols)
    group = lax.axis_index(("tp", "kv"))
    groups = lax.axis_size(("tp", "kv"))
    share = users * length // groups
    group_term = lax.dot_general(
        attended, out_full, (((1,), (1,)), ((), ())), preferred_element_type=jnp.float32
    ).astype(jnp.bfloat16)
    mixed = lax.psum(group_term, ("tp", "kv")).astype(jnp.float32)
    encoded_all = source + mixed
    cross_all = root_norm(encoded_all, cross_gain).astype(jnp.bfloat16)
    encoded_rows = lax.dynamic_slice_in_dim(encoded_all, group * share, share, 0)
    encoded_out = encoded_rows.astype(jnp.bfloat16).reshape(users, share // users, width)
    cross_keys = jnp.dot(cross_all, cross_full[0], preferred_element_type=jnp.float32).astype(
        jnp.bfloat16
    )
    cross_values = jnp.dot(cross_all, cross_full[1], preferred_element_type=jnp.float32).astype(
        jnp.bfloat16
    )
    cross_key_heads = cross_keys.reshape(users, length, key_groups, head_size)
    cross_value_heads = cross_values.reshape(users, length, key_groups, head_size)
    live_events = (
        lax.broadcasted_iota(jnp.int32, (users, length), 1) < (block_counts * BLK)[:, None]
    )
    live_mask = live_events[:, None, None, None, :]
    beam_rows = semantic_ids.shape[1]
    per_user = beam_rows // users
    vocab_rows = code_table.shape[0]
    vocab_ids = group * vocab_rows + lax.broadcasted_iota(jnp.int32, (1, vocab_rows), 1)

    def lookup(id_values):
        onehot = (id_values[:, None] == vocab_ids).astype(jnp.bfloat16)
        return jnp.dot(onehot, code_table, preferred_element_type=jnp.float32)

    def attend(beam_hidden):
        normed_beams = root_norm(beam_hidden, decoder_gain).astype(jnp.bfloat16)
        beam_queries = jnp.dot(
            normed_beams, decoder_query, preferred_element_type=jnp.float32
        ).astype(jnp.bfloat16)
        beam_queries = beam_queries.reshape(users, per_user, key_groups, group_ratio, head_size)
        beam_scores = jnp.einsum(
            "ubgad,ujgd->ugabj", beam_queries, cross_key_heads, preferred_element_type=jnp.float32
        ) * head_size ** (-0.5)
        beam_raised = jnp.where(live_mask, jnp.exp(beam_scores), jnp.float32(0.0))
        beam_total = jnp.sum(beam_raised, axis=-1, keepdims=True)
        beam_soft = (beam_raised / beam_total).astype(jnp.bfloat16)
        beam_attended = jnp.einsum(
            "ugabj,ujgd->ubgad", beam_soft, cross_value_heads, preferred_element_type=jnp.float32
        )
        beam_attended = beam_attended.astype(jnp.bfloat16).reshape(beam_rows, query_cols)
        return lax.dot_general(
            beam_attended, decoder_out, (((1,), (1,)), ((), ())), preferred_element_type=jnp.float32
        )

    def combine(beam_terms):
        return lax.psum(beam_terms.astype(jnp.bfloat16), ("tp", "kv")).astype(jnp.float32)

    local_rows = lax.broadcasted_iota(jnp.int32, (beam_rows,), 0)
    beam_hidden = combine(lookup(semantic_ids[0]))
    mixed_state = attend(beam_hidden)
    for level in range(1, STEPS):
        source_rows = local_rows // per_user * per_user + beam_parents[level - 1]
        moved = jnp.take(mixed_state, source_rows, axis=0) + lookup(semantic_ids[level])
        beam_hidden = jnp.take(beam_hidden, source_rows, axis=0) + combine(moved)
        mixed_state = attend(beam_hidden)
    finished = (beam_hidden + combine(mixed_state)).astype(jnp.bfloat16)
    width_share = width // groups
    beam_out = lax.dynamic_slice_in_dim(finished, group * width_share, width_share, 1)
    return (encoded_out, beam_out)


def solution(mesh):
    in_specs = (
        P("groups", "seq", ("tp", "kv")),
        P(None, ("groups", "seq"), None, ("tp", "kv")),
        P(("groups", "seq")),
        P(None, ("groups", "seq")),
        P(None, ("groups", "seq")),
        P("seq", ("tp", "kv")),
        P(None, "seq", ("tp", "kv")),
        P("seq", ("tp", "kv")),
        P(None, "seq", ("tp", "kv")),
        P(None, ("tp", "kv")),
        P(None, ("tp", "kv")),
        P(("tp", "kv"), None),
        P(),
        P(),
        P(),
    )
    out_specs = (P(("groups", "seq"), ("tp", "kv"), None), P(("groups", "seq"), ("tp", "kv")))
    return jax.shard_map(shards, mesh=mesh, in_specs=in_specs, out_specs=out_specs, check_vma=False)
```

profile of v0, /device:TPU:0, one launch (start us, length us, event | category | flops | bytes accessed | tf_op | source)
XLA Modules:
  0.0 447.2 jit_solution(481606835040528028)
XLA Ops:
  7.2 21.1 %all_to_all.12 = bf16[4,128,512]{2,1,0:T(8,128)(2,1)} all-to-all(bf16[4,128,512]{2,1,0:T(8,128)(2,1)} %param.17), channel_id=1, replica_groups=mesh['groups'=2,'seq'=4,'tp'=2,'kv'=2] {'seq'}, dimensions={0} | all-to-all | bytes 1048576 | tf_op jit(solution)/shard_map/all_to_all | solution.py:38
  28.4 1.1 slice_bitcast_fusion.5
  29.5 1.2 pad_maximum_fusion
  30.8 0.7 all-gather.9.cloned.1.call-update
  32.4 0.9 copy.37
  33.3 0.8 copy.34
  34.1 1.6 fusion.15
  35.7 3.5 convolution_convert_fusion.2
  39.2 11.0 %all-gather.5.cloned.1.call-done = bf16[1,512,2048]{2,1,0:T(8,128)(2,1)} async-done(((bf16[1,512,512]{2,1,0:T(8,128)(2,1)}), bf16[1,512,2048]{2,1,0:T(8,128)(2,1)}) %all-gather.5.cloned.1.call-update) | async-done | bytes 2097168 | tf_op jit(solution)/shard_map/all_gather | solution.py:39
  50.2 2.1 fusion.1
  52.3 80.3 %all-gather.7.cloned.1.call-done = bf16[2048,1024]{1,0:T(8,128)(2,1)} async-done(((bf16[512,1024]{1,0:T(8,128)(2,1)}), bf16[2048,1024]{1,0:T(8,128)(2,1)}) %all-gather.7.cloned.1.call-update) | async-done | bytes 4194320 | tf_op jit(solution)/shard_map/all_gather | solution.py:50
  132.5 5.2 %fusion.16 = bf16[512,1024]{1,0:T(8,128)(2,1)S(1)} fusion(bf16[2048,1024]{1,0:T(8,128)(2,1)} %all-gather.7.cloned.1.call-done, bf16[1,512,2048]{2,1,0:T(8,128)(2,1)} %all-gather.5.cloned.1.call-done, f32[2048]{0:T(1024)S(1)} %copy-done.13, f32[512]{0:T(512)S(1)} %add_rsqrt_fusion.1), kind=kOutput, calls=%fused_computation.35 | convolution fusion | flops 2152202240 | bytes 7350272 | tf_op jit(solution)/shard_map/dot_general | solution.py:48
  137.9 0.8 copy.38
  138.7 0.9 reshape.294
  139.8 3.6 fusion
  143.4 2.4 fusion.19
  145.8 32.5 %all-gather.9.cloned.1.call-done = bf16[2048,512]{1,0:T(8,128)(2,1)} async-done(((bf16[512,512]{1,0:T(8,128)(2,1)}), bf16[2048,512]{1,0:T(8,128)(2,1)}) %all-gather.9.cloned.1.call-update) | async-done | bytes 2097168 | tf_op jit(solution)/shard_map/all_gather | solution.py:57
  178.3 4.2 convolution_convert_fusion
  183.4 50.6 %all-reduce.15.cloned.1.call-done = (bf16[512,2048]{1,0:T(8,128)(2,1)}, bf16[16,2048]{1,0:T(8,128)(2,1)}) async-done(((bf16[512,2048]{1,0:T(8,128)(2,1)}, bf16[16,2048]{1,0:T(8,128)(2,1)}), (bf16[512,2048]{1,0:T(8,128)(2,1)}, bf16[16,2048]{1,0:T(8,128)(2,1)})) %all-reduce.15.cloned.1.call-update) | async-done | bytes 2162704 | tf_op jit(solution)/shard_map/psum | solution.py:93
  234.0 1.0 multiply_reduce_fusion.4
  235.0 2.1 convolution_convert_fusion.12
  237.0 3.0 multiply_reduce_fusion
  240.0 41.1 %all-gather.11.cloned.1.call-done = bf16[2,2048,256]{2,1,0:T(8,128)(2,1)} async-done(((bf16[2,512,256]{2,1,0:T(8,128)(2,1)}), bf16[2,2048,256]{2,1,0:T(8,128)(2,1)}) %all-gather.11.cloned.1.call-update) | async-done | bytes 2097168 | tf_op jit(solution)/shard_map/all_gather | solution.py:58
  281.2 3.8 convolution_convert_fusion.3
  285.6 1.2 convolution_convert_fusion.4
  287.1 0.6 fusion.92
  287.7 0.6 gather_fusion.1
  288.3 3.5 fusion.6
  292.6 29.8 %all-reduce.7.cloned.1.call-done = bf16[16,2048]{1,0:T(8,128)(2,1)} async-done(((bf16[16,2048]{1,0:T(8,128)(2,1)}), bf16[16,2048]{1,0:T(8,128)(2,1)}) %all-reduce.7.cloned.1.call-update) | async-done | bytes 65552 | tf_op jit(solution)/shard_map/psum | solution.py:140
  322.4 1.0 multiply_reduce_fusion.3
  323.5 2.0 convolution_convert_fusion.10
  326.0 0.6 fusion.93
  326.7 0.6 gather_fusion.3
  327.3 3.5 fusion.7
  331.5 31.0 %all-reduce.9.cloned.1.call-done = bf16[16,2048]{1,0:T(8,128)(2,1)} async-done(((bf16[16,2048]{1,0:T(8,128)(2,1)}), bf16[16,2048]{1,0:T(8,128)(2,1)}) %all-reduce.9.cloned.1.call-update) | async-done | bytes 65552 | tf_op jit(solution)/shard_map/psum | solution.py:140
  362.5 1.0 multiply_reduce_fusion.2
  363.6 2.0 convolution_convert_fusion.8
  366.2 0.6 fusion.94
  366.8 0.6 gather_fusion.5
  367.4 3.5 fusion.8
  371.0 4.4 convert_add_fusion
  376.1 26.6 %all-reduce.11.cloned.1.call-done = bf16[16,2048]{1,0:T(8,128)(2,1)} async-done(((bf16[16,2048]{1,0:T(8,128)(2,1)}), bf16[16,2048]{1,0:T(8,128)(2,1)}) %all-reduce.11.cloned.1.call-update) | async-done | bytes 65552 | tf_op jit(solution)/shard_map/psum | solution.py:140
  402.7 1.0 multiply_reduce_fusion.1
  403.7 2.0 convolution_convert_fusion.6
  406.3 1.3 convolution_convert_fusion.1
  407.6 1.9 fusion.42
  409.5 29.8 %all-reduce.13.cloned.1.call-done = bf16[16,2048]{1,0:T(8,128)(2,1)} async-done(((bf16[16,2048]{1,0:T(8,128)(2,1)}), bf16[16,2048]{1,0:T(8,128)(2,1)}) %all-reduce.13.cloned.1.call-update) | async-done | bytes 65552 | tf_op jit(solution)/shard_map/psum | solution.py:140
  439.3 1.3 fusion.66
  (92 shorter events, 6.2 us)
Async XLA Ops:
  7.2 279.9 %copy-start = (bf16[2048,512]{1,0:T(8,128)(2,1)S(1)}, bf16[2048,512]{1,0:T(8,128)(2,1)}, u32[]{:S(2)}) copy-start(bf16[2048,512]{1,0:T(8,128)(2,1)} %param.27) | copy-start | bytes 6291460
  7.2 22.3 %copy-start.6 = (bf16[512,512]{1,0:T(8,128)(2,1)S(1)}, bf16[512,512]{1,0:T(8,128)(2,1)}, u32[]{:S(2)}) copy-start(bf16[512,512]{1,0:T(8,128)(2,1)} %param.22) | copy-start | bytes 1572868
  7.2 43.0 %all-gather.5.cloned.1.call-start = ((), (), s32[]{:S(2)}) async-start(), calls=%async_computation.1 | async-start | bytes 2621440 | tf_op jit(solution)/shard_map/all_gather | solution.py:39
  28.3 104.2 %all-gather.7.cloned.1.call-start = ((), (), s32[]{:S(2)}) async-start(), calls=%async_computation.2 | async-start | bytes 5242880 | tf_op jit(solution)/shard_map/all_gather | solution.py:50
  29.5 2.7 copy-start.4
  30.7 3.4 copy-start.10
  30.7 147.6 %all-gather.9.cloned.1.call-start = ((), (), s32[]{:S(2)}) async-start(), calls=%async_computation.3 | async-start | bytes 2621440 | tf_op jit(solution)/shard_map/all_gather | solution.py:57
  31.5 202.5 %all-reduce.15.cloned.1.call-start = ((), (), s32[]{:S(2)}) async-start(), calls=%async_computation.9 | async-start | bytes 4325376 | tf_op jit(solution)/shard_map/psum | solution.py:93
  39.2 93.3 %copy-start.13 = (f32[2048]{0:T(1024)S(1)}, f32[2048]{0:T(1024)}, u32[]{:S(2)}) copy-start(f32[2048]{0:T(1024)} %param.29) | copy-start | bytes 24580
  137.9 1.9 copy-start.8
  139.8 3.6 copy-start.5
  139.8 3.6 copy-start.7
  182.5 0.9 copy-start.11
  182.5 52.4 %copy-start.9 = (f32[2048]{0:T(1024)S(1)}, f32[2048]{0:T(1024)}, u32[]{:S(2)}) copy-start(f32[2048]{0:T(1024)} %param.31) | copy-start | bytes 24580
  182.5 98.6 %all-gather.11.cloned.1.call-start = ((), (), s32[]{:S(2)}) async-start(), calls=%async_computation.4 | async-start | bytes 2621440 | tf_op jit(solution)/shard_map/all_gather | solution.py:58
  183.1 139.3 %all-reduce.7.cloned.1.call-start = ((), (), s32[]{:S(2)}) async-start(), calls=%async_computation.5 | async-start | bytes 131072 | tf_op jit(solution)/shard_map/psum | solution.py:140
  237.0 44.1 %copy-start.14 = (f32[2048]{0:T(1024)S(1)}, f32[2048]{0:T(1024)}, u32[]{:S(2)}) copy-start(f32[2048]{0:T(1024)} %param.30) | copy-start | bytes 24580
  281.2 4.0 copy-start.1
  281.2 4.0 copy-start.2
  281.2 4.4 copy-start.12
  288.3 3.6 copy-start.3
  291.9 70.6 %all-reduce.9.cloned.1.call-start = ((), (), s32[]{:S(2)}) async-start(), calls=%async_computation.6 | async-start | bytes 131072 | tf_op jit(solution)/shard_map/psum | solution.py:140
  330.8 71.8 %all-reduce.11.cloned.1.call-start = ((), (), s32[]{:S(2)}) async-start(), calls=%async_computation.7 | async-start | bytes 131072 | tf_op jit(solution)/shard_map/psum | solution.py:140
  371.0 68.3 %all-reduce.13.cloned.1.call-start = ((), (), s32[]{:S(2)}) async-start(), calls=%async_computation.8 | async-start | bytes 131072 | tf_op jit(solution)/shard_map/psum | solution.py:140
Sparse Core Ops, SparseCore 0:
  28.5 21.6 all-gather.4
  51.8 80.7 all-gather.6
  134.1 44.1 all-gather.8
  182.7 51.2 all-reduce.14
  235.4 45.7 all-gather.10
  292.0 30.3 all-reduce.6
  331.0 31.5 all-reduce.8
  371.1 31.5 all-reduce.10
  407.7 31.5 all-reduce.12
where the time goes:
time: 448 us; the launch traced here: 447 us
  waiting for transfers between devices  334 us (75%)
  matrix products  47.6 us (11%)
  blocking collectives  21.1 us (5%)
  other arithmetic  17.9 us (4%)
  between operations  14.9 us (3%)
  local copies, waits for them, and re-layouts  11.2 us (2%)
    psum x4, waiting for transfers between devices, combine(): lax.psum(beam_terms.astype(jnp.bfloat16), ('tp', 'kv')).astype(jnp.float32)  117 us
    all_gather x1, waiting for transfers between devices, shards(): lax.all_gather(joined, 'seq', axis=0, tiled=True)  80.3 us
    psum x1, waiting for transfers between devices, shards(): mixed = lax.psum(group_term, ('tp', 'kv')).astype(jnp.float32)  50.6 us
    all_gather x1, waiting for transfers between devices, shards(): lax.all_gather(cross_weight, 'seq', axis=1, tiled=True)  41.1 us
    all_gather x1, waiting for transfers between devices, shards(): lax.all_gather(out_weight, 'seq', axis=0, tiled=True)  32.5 us
    all_to_all x1, blocking collectives, shards(): lax.all_to_all(events, 'seq', split_axis=0, concat_axis=1, tiled=True)  21.1 us
    dot_general x4, matrix products, lookup(): return jnp.dot(onehot, code_table, preferred_element_type=jnp.float32)  14.1 us
    all_gather x1, waiting for transfers between devices, shards(): whole = lax.all_gather(relayed, ('tp', 'kv'), axis=2, tiled=True)  11 us
  transfers between devices with their start and end apart: 9, of which 9 were waited for; matrix products, arithmetic and copies ran while one was open for 9% of the time, Pallas kernels for 0%

commit v1 on v0

--- a/solution.py
+++ b/solution.py
@@ -137,7 +137,9 @@
         )
 
     def combine(beam_terms):
-        return lax.psum(beam_terms.astype(jnp.bfloat16), ("tp", "kv")).astype(jnp.float32)
+        return jnp.sum(
+            lax.all_gather(beam_terms.astype(jnp.bfloat16), ("tp", "kv")), axis=0
+        ).astype(jnp.float32)
 
     local_rows = lax.broadcasted_iota(jnp.int32, (beam_rows,), 0)
     beam_hidden = combine(lookup(semantic_ids[0]))

time: 448 us -> 345 us (0.77)
  waiting for transfers between devices: 334 us -> 210 us
  blocking collectives: 21.1 us -> 52.3 us
  other arithmetic: 17.9 us -> 12.5 us
    psum x4 -> x0, waiting for transfers between devices: 117 us -> none  [combine(): lax.psum(beam_terms.astype(jnp.bfloat16), ('tp', 'kv')).astype(jnp.float32)]
    all_gather x0 -> x5, blocking collectives: none -> 31.2 us  [combine(): lax.all_gather(beam_terms.astype(jnp.bfloat16), ('tp', 'kv'))]
    psum x1, waiting for transfers between devices: 50.6 us -> 36.8 us  [shards(): mixed = lax.psum(group_term, ('tp', 'kv')).astype(jnp.float32)]
  transfers between devices with their start and end apart: 9 -> 5, of which waited for: 9 -> 5; matrix products, arithmetic and copies ran while one was open for 9% -> 9% of each run, Pallas kernels for 0% -> 0%
where the time goes in v1:
time: 345 us; the launch traced here: 344 us
  waiting for transfers between devices  210 us (61%)
  blocking collectives  52.3 us (15%)
  matrix products  44.4 us (13%)
  between operations  14.9 us (4%)
  other arithmetic  12.5 us (4%)
  local copies, waits for them, and re-layouts  10.2 us (3%)
    all_gather x1, waiting for transfers between devices, shards(): lax.all_gather(joined, 'seq', axis=0, tiled=True)  80.3 us
    all_gather x1, waiting for transfers between devices, shards(): lax.all_gather(cross_weight, 'seq', axis=1, tiled=True)  44.2 us
    psum x1, waiting for transfers between devices, shards(): mixed = lax.psum(group_term, ('tp', 'kv')).astype(jnp.float32)  36.8 us
    all_gather x1, waiting for transfers between devices, shards(): lax.all_gather(out_weight, 'seq', axis=0, tiled=True)  32.6 us
    all_gather x5, blocking collectives, combine(): lax.all_gather(beam_terms.astype(jnp.bfloat16), ('tp', 'kv'))  31.2 us
    all_to_all x1, blocking collectives, shards(): lax.all_to_all(events, 'seq', split_axis=0, concat_axis=1, tiled=True)  21.1 us
    all_gather x1, waiting for transfers between devices, shards(): whole = lax.all_gather(relayed, ('tp', 'kv'), axis=2, tiled=True)  14.5 us
    dot_general x4, matrix products, lookup(): return jnp.dot(onehot, code_table, preferred_element_type=jnp.float32)  11.6 us
  transfers between devices with their start and end apart: 5, of which 5 were waited for; matrix products, arithmetic and copies ran while one was open for 9% of the time, Pallas kernels for 0%

profile of v1, /device:TPU:0, one launch (start us, length us, event | category | flops | bytes accessed | tf_op | source)
XLA Modules:
  0.0 344.0 jit_solution(4878761425732444620)
XLA Ops:
  7.2 21.1 %all_to_all.12 = bf16[4,128,512]{2,1,0:T(8,128)(2,1)} all-to-all(bf16[4,128,512]{2,1,0:T(8,128)(2,1)} %param.17), channel_id=1, replica_groups=mesh['groups'=2,'seq'=4,'tp'=2,'kv'=2] {'seq'}, dimensions={0} | all-to-all | bytes 1048576 | tf_op jit(solution)/shard_map/all_to_all | solution.py:38
  28.4 1.1 slice_bitcast_fusion.5
  29.5 1.2 pad_maximum_fusion
  30.8 0.7 all-gather.14.cloned.1.call-update
  32.4 0.9 copy.37
  33.3 0.9 copy.34
  34.1 1.6 fusion.15
  35.7 14.5 %all-gather.10.cloned.1.call-done = bf16[1,512,2048]{2,1,0:T(8,128)(2,1)} async-done(((bf16[1,512,512]{2,1,0:T(8,128)(2,1)}), bf16[1,512,2048]{2,1,0:T(8,128)(2,1)}) %all-gather.10.cloned.1.call-update) | async-done | bytes 2097168 | tf_op jit(solution)/shard_map/all_gather | solution.py:39
  50.2 2.1 fusion.1
  52.3 80.3 %all-gather.12.cloned.1.call-done = bf16[2048,1024]{1,0:T(8,128)(2,1)} async-done(((bf16[512,1024]{1,0:T(8,128)(2,1)}), bf16[2048,1024]{1,0:T(8,128)(2,1)}) %all-gather.12.cloned.1.call-update) | async-done | bytes 4194320 | tf_op jit(solution)/shard_map/all_gather | solution.py:50
  132.5 5.2 %fusion.16 = bf16[512,1024]{1,0:T(8,128)(2,1)S(1)} fusion(bf16[2048,1024]{1,0:T(8,128)(2,1)} %all-gather.12.cloned.1.call-done, bf16[1,512,2048]{2,1,0:T(8,128)(2,1)} %all-gather.10.cloned.1.call-done, f32[2048]{0:T(1024)S(1)} %copy-done.12, f32[512]{0:T(512)S(1)} %add_rsqrt_fusion.1), kind=kOutput, calls=%fused_computation.35 | convolution fusion | flops 2152202240 | bytes 7350272 | tf_op jit(solution)/shard_map/dot_general | solution.py:48
  137.9 0.7 copy.38
  138.7 0.9 reshape.294
  139.7 3.6 %fusion = (f32[2,2,512]{2,1,0:T(2,128)S(1)}, f32[2,1024,512,2]{2,1,3,0:T(8,128)S(1)}) fusion(pred[512,1024]{0,1:T(8,128)(4,1)} %fusion.15, bf16[512,2,2,128]{3,2,1,0:T(2,128)(2,1)} %reshape.294, bf16[1,512,2,128]{3,1,2,0:T(8,128)(2,1)} %copy.38, bf16[1,512,2,128]{3,1,2,0:T(8,128)(2,1)S(1)} %copy-done.7), kind=kOutput, calls=%fused_computation.8 | convolution fusion | flops 544208896 | bytes 9969664 | tf_op jit(solution)/shard_map/uigad,ujgd->ugaij/dot_general | solution.py:71
  143.3 2.4 fusion.19
  145.7 32.6 %all-gather.14.cloned.1.call-done = bf16[2048,512]{1,0:T(8,128)(2,1)} async-done(((bf16[512,512]{1,0:T(8,128)(2,1)}), bf16[2048,512]{1,0:T(8,128)(2,1)}) %all-gather.14.cloned.1.call-update) | async-done | bytes 2097168 | tf_op jit(solution)/shard_map/all_gather | solution.py:57
  178.3 4.2 %convolution_convert_fusion = bf16[512,2048]{1,0:T(8,128)(2,1)} fusion(bf16[512,512]{0,1:T(8,128)(2,1)S(1)} %bitcast.216, bf16[2048,512]{1,0:T(8,128)(2,1)} %all-gather.14.cloned.1.call-done), kind=kOutput, calls=%fused_computation.19 | convolution fusion | flops 1074790400 | bytes 4718592 | tf_op jit(solution)/shard_map/dot_general | solution.py:90
  183.2 2.9 convolution_convert_fusion.2
  186.1 7.9 %all-gather = bf16[64,2048]{1,0:T(8,128)(2,1)S(1)} all-gather(bf16[16,2048]{1,0:T(8,128)(2,1)S(1)} %convolution_convert_fusion.2), channel_id=2, replica_groups=mesh['groups'=2,'seq'=4,'tp'=2,'kv'=2] {'tp','kv'}, dimensions={0}, use_global_device_ids=true | all-gather | bytes 327680 | tf_op jit(solution)/shard_map/all_gather | solution.py:141
  194.2 2.0 convolution_convert_fusion.12
  196.3 0.6 gather_fusion
  196.9 36.8 %all-reduce.2.cloned.1.call-done = bf16[512,2048]{1,0:T(8,128)(2,1)} async-done(((bf16[512,2048]{1,0:T(8,128)(2,1)}), bf16[512,2048]{1,0:T(8,128)(2,1)}) %all-reduce.2.cloned.1.call-update) | async-done | bytes 2097168 | tf_op jit(solution)/shard_map/psum | solution.py:93
  233.8 3.0 multiply_reduce_fusion
  236.7 44.2 %all-gather.16.cloned.1.call-done = bf16[2,2048,256]{2,1,0:T(8,128)(2,1)} async-done(((bf16[2,512,256]{2,1,0:T(8,128)(2,1)}), bf16[2,2048,256]{2,1,0:T(8,128)(2,1)}) %all-gather.16.cloned.1.call-update) | async-done | bytes 2097168 | tf_op jit(solution)/shard_map/all_gather | solution.py:58
  281.0 3.8 %convolution_convert_fusion.3 = bf16[512,256]{0,1:T(8,128)(2,1)S(1)} fusion(bf16[2,2048,256]{2,1,0:T(8,128)(2,1)} %all-gather.16.cloned.1.call-done, f32[2048]{0:T(1024)S(1)} %copy-done.13, f32[512]{0:T(512)S(1)} %add_rsqrt_fusion, bf16[512,2048]{1,0:T(8,128)(2,1)} %all-reduce.2.cloned.1.call-done, bf16[1,512,2048]{2,1,0:T(8,128)(2,1)} %all-gather.10.cloned.1.call-done), kind=kOutput, calls=%fused_computation.37 | convolution fusion | flops 543293440 | bytes 5515264 | tf_op jit(solution)/shard_map/dot_general | solution.py:98
  285.4 1.2 convolution_convert_fusion.4
  286.8 0.6 fusion.92
  287.5 0.6 gather_fusion.1
  288.1 2.9 fusion.6
  291.0 5.8 %all-gather.1 = bf16[64,2048]{1,0:T(8,128)(2,1)S(1)} all-gather(bf16[16,2048]{1,0:T(8,128)(2,1)S(1)} %fusion.6), channel_id=3, replica_groups=mesh['groups'=2,'seq'=4,'tp'=2,'kv'=2] {'tp','kv'}, dimensions={0}, use_global_device_ids=true | all-gather | bytes 327680 | tf_op jit(solution)/shard_map/all_gather | solution.py:141
  297.0 2.0 convolution_convert_fusion.10
  299.6 0.6 fusion.93
  300.2 0.6 gather_fusion.2
  300.9 0.6 gather_fusion.3
  301.5 2.9 fusion.7
  304.4 5.8 %all-gather.2 = bf16[64,2048]{1,0:T(8,128)(2,1)S(1)} all-gather(bf16[16,2048]{1,0:T(8,128)(2,1)S(1)} %fusion.7), channel_id=4, replica_groups=mesh['groups'=2,'seq'=4,'tp'=2,'kv'=2] {'tp','kv'}, dimensions={0}, use_global_device_ids=true | all-gather | bytes 327680 | tf_op jit(solution)/shard_map/all_gather | solution.py:141
  310.5 2.0 convolution_convert_fusion.8
  313.0 0.6 fusion.94
  313.7 0.6 gather_fusion.4
  314.3 0.6 gather_fusion.5
  314.9 2.9 fusion.8
  317.8 5.8 %all-gather.3 = bf16[64,2048]{1,0:T(8,128)(2,1)S(1)} all-gather(bf16[16,2048]{1,0:T(8,128)(2,1)S(1)} %fusion.8), channel_id=5, replica_groups=mesh['groups'=2,'seq'=4,'tp'=2,'kv'=2] {'tp','kv'}, dimensions={0}, use_global_device_ids=true | all-gather | bytes 327680 | tf_op jit(solution)/shard_map/all_gather | solution.py:141
  323.9 2.0 convolution_convert_fusion.6
  326.5 0.6 convolution_convert_fusion.1
  327.1 5.9 %all-gather.4 = bf16[64,2048]{1,0:T(8,128)(2,1)S(1)} all-gather(bf16[16,2048]{1,0:T(8,128)(2,1)S(1)} %convolution_convert_fusion.1), channel_id=6, replica_groups=mesh['groups'=2,'seq'=4,'tp'=2,'kv'=2] {'tp','kv'}, dimensions={0}, use_global_device_ids=true | all-gather | bytes 327680 | tf_op jit(solution)/shard_map/all_gather | solution.py:141
  333.0 0.6 fusion.66
  333.6 3.0 convert_add_fusion
  336.7 0.8 fusion.42
  (88 shorter events, 5.0 us)
Async XLA Ops:
  7.2 279.7 %copy-start = (bf16[2048,512]{1,0:T(8,128)(2,1)S(1)}, bf16[2048,512]{1,0:T(8,128)(2,1)}, u32[]{:S(2)}) copy-start(bf16[2048,512]{1,0:T(8,128)(2,1)} %param.27) | copy-start | bytes 6291460
  7.2 22.3 %copy-start.5 = (bf16[512,512]{1,0:T(8,128)(2,1)S(1)}, bf16[512,512]{1,0:T(8,128)(2,1)}, u32[]{:S(2)}) copy-start(bf16[512,512]{1,0:T(8,128)(2,1)} %param.22) | copy-start | bytes 1572868
  7.2 43.0 %all-gather.10.cloned.1.call-start = ((), (), s32[]{:S(2)}) async-start(), calls=%async_computation.1 | async-start | bytes 2621440 | tf_op jit(solution)/shard_map/all_gather | solution.py:39
  28.3 104.2 %all-gather.12.cloned.1.call-start = ((), (), s32[]{:S(2)}) async-start(), calls=%async_computation.2 | async-start | bytes 5242880 | tf_op jit(solution)/shard_map/all_gather | solution.py:50
  29.5 2.7 copy-start.3
  30.7 147.6 %all-gather.14.cloned.1.call-start = ((), (), s32[]{:S(2)}) async-start(), calls=%async_computation.3 | async-start | bytes 2621440 | tf_op jit(solution)/shard_map/all_gather | solution.py:57
  31.5 202.3 %all-reduce.2.cloned.1.call-start = ((), (), s32[]{:S(2)}) async-start(), calls=%async_computation.4 | async-start | bytes 4194304 | tf_op jit(solution)/shard_map/psum | solution.py:93
  32.2 100.3 %copy-start.12 = (f32[2048]{0:T(1024)S(1)}, f32[2048]{0:T(1024)}, u32[]{:S(2)}) copy-start(f32[2048]{0:T(1024)} %param.29) | copy-start | bytes 24580
  137.9 1.8 copy-start.7
  139.7 3.6 %copy-start.4 = (pred[512,1024]{0,1:T(8,128)(4,1)S(1)}, pred[512,1024]{0,1:T(8,128)(4,1)}, u32[]{:S(2)}) copy-start(pred[512,1024]{0,1:T(8,128)(4,1)} %fusion.15) | copy-start | bytes 1572868
  139.7 3.6 %copy-start.6 = (bf16[1,1,512,256]{2,3,1,0:T(8,128)(2,1)S(1)}, bf16[1,1,512,256]{2,3,1,0:T(8,128)(2,1)}, u32[]{:S(2)}) copy-start(bf16[1,1,512,256]{2,3,1,0:T(8,128)(2,1)} %copy.34) | copy-start | bytes 786436
  182.5 0.7 copy-start.9
  182.5 98.4 %all-gather.16.cloned.1.call-start = ((), (), s32[]{:S(2)}) async-start(), calls=%async_computation.5 | async-start | bytes 2621440 | tf_op jit(solution)/shard_map/all_gather | solution.py:58
  183.2 11.0 %copy-start.8 = (f32[2048]{0:T(1024)S(1)}, f32[2048]{0:T(1024)}, u32[]{:S(2)}) copy-start(f32[2048]{0:T(1024)} %param.31) | copy-start | bytes 24580
  186.1 10.2 %copy-start.10 = (s32[3,16]{1,0:T(4,128)S(1)}, s32[3,16]{1,0:T(4,128)}, u32[]{:S(2)}) copy-start(s32[3,16]{1,0:T(4,128)} %param.21) | copy-start | bytes 580
  196.9 84.0 %copy-start.13 = (f32[2048]{0:T(1024)S(1)}, f32[2048]{0:T(1024)}, u32[]{:S(2)}) copy-start(f32[2048]{0:T(1024)} %param.30) | copy-start | bytes 24580
  280.9 4.0 %copy-start.1 = (bf16[1,512,2048]{2,1,0:T(8,128)(2,1)S(1)}, bf16[1,512,2048]{2,1,0:T(8,128)(2,1)}, u32[]{:S(2)}) copy-start(bf16[1,512,2048]{2,1,0:T(8,128)(2,1)} %all-gather.10.cloned.1.call-done) | copy-start | bytes 6291460
  280.9 4.0 %copy-start.2 = (bf16[512,2048]{1,0:T(8,128)(2,1)S(1)}, bf16[512,2048]{1,0:T(8,128)(2,1)}, u32[]{:S(2)}) copy-start(bf16[512,2048]{1,0:T(8,128)(2,1)} %all-reduce.2.cloned.1.call-done) | copy-start | bytes 6291460
  280.9 4.4 %copy-start.11 = (bf16[2,2048,256]{2,1,0:T(8,128)(2,1)S(1)}, bf16[2,2048,256]{2,1,0:T(8,128)(2,1)}, u32[]{:S(2)}) copy-start(bf16[2,2048,256]{2,1,0:T(8,128)(2,1)} %all-gather.16.cloned.1.call-done) | copy-start | bytes 6291460
Sparse Core Ops, SparseCore 0:
  28.5 21.6 all-gather.9
  51.8 80.7 all-gather.11
  134.1 44.1 all-gather.13
  182.6 51.0 all-reduce.1
  235.2 45.7 all-gather.15
